TPU v7x, 512 devices: a whole 4x4x16 slice. The times are simulated.
512 devices in a mesh: dp: 32 (over z, core), tensor: 16 (over y, x).
Axes of the slice: x: 4, y: 4, z: 16, core: 2. Of those that a mesh axis runs over, the one named last changes fastest.
Arguments:
- dout: bfloat16 [12288, 5120], P(('dp', 'tensor')), may hold values from -0.75 to 0.75
- attn_ctx: bfloat16 [12288, 5120], P('dp', 'tensor'), may hold values from -6 to 6
- mlp_hidden: bfloat16 [12288, 13824], P('dp', 'tensor'), may hold values from -6 to 6
- w_out: bfloat16 [5120, 5120], P('tensor', 'dp'), may hold values from -0.078125 to 0.078125
- w_down: bfloat16 [13824, 5120], P('tensor', 'dp'), may hold values from -0.0546875 to 0.0546875
- head_logits: float32 [40], replicated, may hold values from -2 to 3
- unit_logits: float32 [13824], P('tensor'), may hold values from -2 to 3
- head_noise: float32 [40], replicated, may hold values from 0.001 to 0.999
- unit_noise: float32 [13824], P('tensor'), may hold values from 0.001 to 0.999
- linear_mult: float32 [1], replicated, may hold values from 100 to 300
- square_mult: float32 [1], replicated, may hold values from 1 to 4
- target: float32 [1], replicated, may hold values from 40 to 70
Outputs:
- ctx_grad: bfloat16 [12288, 5120], P('dp', 'tensor')
- hidden_grad: bfloat16 [12288, 13824], P('dp', 'tensor')
- head_grad: float32 [40], replicated
- unit_grad: float32 [13824], P('tensor')
All inputs are finite; a program needn't handle non-finite values.
Results may differ from a plain program's by a relative error of at most 0.001.
Values may be sent and summed in bfloat16 or wider, within the bound.
No kernel may reach another device: no remote copies, remote signals or barrier semaphores. Data moves between devices by JAX's collectives and lax.ppermute only.
A program may use at most 64 MiB of HBM per device.

v0:
```python
import jax
import jax.numpy as jnp
from jax import lax
from jax.sharding import PartitionSpec as P

H = 40
HEAD = 128
FF = 13824
low_end = -0.1
high_end = 1.1
temper = 2.0 / 3.0


def concrete(logits, noise):
    shape_s = jax.nn.sigmoid((jnp.log(noise) - jnp.log(1.0 - noise) + logits) / temper)
    stretched = shape_s * (high_end - low_end) + low_end
    gate = jnp.clip(stretched, 0.0, 1.0)
    inside = jnp.logical_and(stretched > 0.0, stretched < 1.0)
    slope = jnp.where(
        inside, (high_end - low_end) / temper * shape_s * (1.0 - shape_s), 0.0 * shape_s
    )
    return (gate, slope)


def open_prob(logits):
    return jax.nn.sigmoid(logits - temper * jnp.log(-low_end / high_end))


def local(
    dout,
    attn_ctx,
    mlp_hidden,
    w_out,
    w_down,
    head_logits,
    unit_logits,
    head_noise,
    unit_noise,
    linear_mult,
    square_mult,
    target,
):
    head_gate, head_slope = concrete(head_logits, head_noise)
    unit_gate, unit_slope = concrete(unit_logits, unit_noise)
    col_count = attn_ctx.shape[1]
    head_total = head_logits.shape[0]
    tensor_index = lax.axis_index("tensor")
    columns = tensor_index * col_count + lax.iota(jnp.int32, col_count)
    owner = columns // HEAD
    member = (owner[:, None] == lax.iota(jnp.int32, head_total)[None, :]).astype(jnp.float32)
    col_gate = jnp.dot(member, head_gate, precision=lax.Precision.HIGHEST)
    full_rows = lax.all_gather(dout, "tensor", axis=0, tiled=True)
    dims = (((1,), (1,)), ((), ()))

    def contract(piece):
        return lax.dot_general(full_rows, piece, dims, preferred_element_type=jnp.float32)

    ctx_pre = contract(lax.all_gather(w_out, "dp", axis=1, tiled=True))
    hid_pre = contract(lax.all_gather(w_down, "dp", axis=1, tiled=True))
    ctx_grad = (ctx_pre * col_gate[None, :]).astype(jnp.bfloat16)
    hidden_grad = (hid_pre * unit_gate[None, :]).astype(jnp.bfloat16)
    col_part = jnp.sum(attn_ctx.astype(jnp.float32) * ctx_pre, axis=0)
    unit_part = jnp.sum(mlp_hidden.astype(jnp.float32) * hid_pre, axis=0)
    head_part = jnp.dot(col_part, member, precision=lax.Precision.HIGHEST)
    p_head = open_prob(head_logits)
    p_unit = open_prob(unit_logits)
    local_mass = jnp.sum(p_unit)
    unit_data = lax.psum(unit_part, "dp")
    head_data = lax.psum(head_part, ("dp", "tensor"))
    unit_mass = lax.psum(local_mass, "tensor")
    denom = 4.0 * HEAD * H + 3.0 * FF
    size = 100.0 * (4.0 * HEAD * jnp.sum(p_head) + 3.0 * unit_mass) / denom
    factor = linear_mult[0] + 2.0 * square_mult[0] * (size - target[0])
    head_grad = head_data * head_slope + factor * (400.0 * HEAD / denom) * p_head * (1.0 - p_head)
    unit_grad = unit_data * unit_slope + factor * (300.0 / denom) * p_unit * (1.0 - p_unit)
    return (ctx_grad, hidden_grad, head_grad, unit_grad)


def solution(mesh):
    placed = (
        P(("dp", "tensor"), None),
        P("dp", "tensor"),
        P("dp", "tensor"),
        P("tensor", "dp"),
        P("tensor", "dp"),
        P(),
        P("tensor"),
        P(),
        P("tensor"),
        P(),
        P(),
        P(),
    )
    return jax.shard_map(
        local,
        mesh=mesh,
        in_specs=placed,
        out_specs=(P("dp", "tensor"), P("dp", "tensor"), P(), P("tensor")),
        check_vma=False,
    )
```

profile of v0, /device:TPU:1, one launch (start us, length us, event | category | flops | bytes accessed | tf_op | source)
XLA Modules:
  0.0 329.6 jit_solution(5489138382124432926)
XLA Ops:
  7.2 0.0 all-gather.6.cloned.1.call-start
  7.2 0.7 all-gather.6.cloned.1.call-update
  7.9 0.0 all-gather.4.cloned.1.call-start
  7.9 0.7 all-gather.4.cloned.1.call-update
  8.6 0.0 all-gather.8.cloned.1.call-start
  8.7 0.7 all-gather.8.cloned.1.call-update
  9.4 1.3 fusion.2
  10.7 34.9 %psum.22 = f32[]{:T(128)} all-reduce(f32[]{:T(128)} %get-tuple-element.11), channel_id=1, replica_groups=mesh['dp'=32,'tensor'=16] {'tensor'}, use_global_device_ids=true, to_apply=%region_4.5 | all-reduce | flops 1 | bytes 8 | tf_op jit(solution)/shard_map/psum | solution.py:70
  48.2 1.3 fusion.17
  50.1 0.0 copy-start.2
  50.1 0.0 copy-start.3
  50.2 0.0 copy-start.4
  50.2 38.7 %all-gather.6.cloned.1.call-done = bf16[320,5120]{0,1:T(8,128)(2,1)} async-done(((bf16[320,160]{0,1:T(8,128)(2,1)}), bf16[320,5120]{0,1:T(8,128)(2,1)}) %all-gather.6.cloned.1.call-update) | async-done | bytes 3276816 | tf_op jit(solution)/shard_map/all_gather | solution.py:58
  88.8 65.0 %all-gather.4.cloned.1.call-done = bf16[384,5120]{1,0:T(8,128)(2,1)} async-done(((bf16[24,5120]{1,0:T(8,128)(2,1)}), bf16[384,5120]{1,0:T(8,128)(2,1)}) %all-gather.4.cloned.1.call-update) | async-done | bytes 3932176 | tf_op jit(solution)/shard_map/all_gather | solution.py:52
  153.9 5.3 %multiply_reduce_fusion.1 = (f32[320]{0:T(512)S(1)}, f32[384,320]{0,1:T(8,128)S(1)}) fusion(bf16[384,320]{0,1:T(8,128)(2,1)} %param.13, bf16[384,5120]{1,0:T(8,128)(2,1)} %all-gather.4.cloned.1.call-done, bf16[320,5120]{0,1:T(8,128)(2,1)} %all-gather.6.cloned.1.call-done), kind=kOutput, calls=%fused_computation.4 | convolution fusion | flops 1258659584 | bytes 7947520 | tf_op jit(solution)/shard_map/dot_general | solution.py:56
  159.2 0.2 convolution_bitcast_fusion
  159.5 105.0 %psum.21 = f32[40]{0:T(128)S(1)} all-reduce(f32[40]{0:T(128)S(1)} %convolution_bitcast_fusion), channel_id=1, replica_groups=mesh['dp'=32,'tensor'=16] {'dp','tensor'}, use_global_device_ids=true, to_apply=%region_1.2 | all-reduce | flops 40 | bytes 320 | tf_op jit(solution)/shard_map/psum | solution.py:69
  264.5 0.0 copy-done.2
  264.5 0.0 copy-done.3
  264.5 0.5 multiply_add_fusion.2
  265.0 0.3 convolution_reduce_fusion
  265.3 0.8 multiply_convert_fusion.1
  266.1 0.0 all-gather.8.cloned.1.call-done
  266.2 0.0 copy-done.4
  266.2 0.0 copy-start
  266.2 0.0 copy-start.1
  266.2 10.5 %multiply_reduce_fusion = (f32[864]{0:T(1024)S(1)}, bf16[384,864]{0,1:T(8,128)(2,1)}) fusion(bf16[384,864]{0,1:T(8,128)(2,1)S(1)} %copy-done.4, f32[864]{0:T(1024)S(1)} %get-tuple-element.10, bf16[384,5120]{1,0:T(8,128)(2,1)} %all-gather.4.cloned.1.call-done, bf16[864,5120]{0,1:T(8,128)(2,1)} %all-gather.8.cloned.1.call-done), kind=kOutput, calls=%fused_computation | convolution fusion | flops 3399044352 | bytes 14113536 | tf_op jit(solution)/shard_map/dot_general | solution.py:56
  276.7 45.8 %psum.23 = f32[864]{0:T(1024)S(1)} all-reduce(f32[864]{0:T(1024)S(1)} %get-tuple-element.8), channel_id=1, replica_groups=mesh['dp'=32,'tensor'=16] {'dp'}, use_global_device_ids=true, to_apply=%region_6.7 | all-reduce | flops 864 | bytes 6912 | tf_op jit(solution)/shard_map/psum | solution.py:68
  322.5 0.0 copy-done
  322.5 0.0 copy-done.1
  322.5 0.6 multiply_add_fusion
  (2 shorter events, 0.0 us)
Async XLA Ops:
  7.2 81.7 %all-gather.6.cloned.1.call-start = ((), (), s32[]{:S(2)}) async-start(), calls=%async_computation.1 | async-start | bytes 4055040 | tf_op jit(solution)/shard_map/all_gather | solution.py:58
  7.9 146.0 %all-gather.4.cloned.1.call-start = ((), (), s32[]{:S(2)}) async-start(), calls=%async_computation | async-start | bytes 4177920 | tf_op jit(solution)/shard_map/all_gather | solution.py:52
  8.6 257.5 %all-gather.8.cloned.1.call-start = ((), (), s32[]{:S(2)}) async-start(), calls=%async_computation.2 | async-start | bytes 9461760 | tf_op jit(solution)/shard_map/all_gather | solution.py:59
  50.1 214.4 %copy-start.2 = (f32[40]{0:T(128)S(1)}, f32[40]{0:T(128)}, u32[]{:S(2)}) copy-start(f32[40]{0:T(128)} %param.17) | copy-start | bytes 484
  50.1 214.4 %copy-start.3 = (f32[40]{0:T(128)S(1)}, f32[40]{0:T(128)}, u32[]{:S(2)}) copy-start(f32[40]{0:T(128)} %param.19) | copy-start | bytes 484
  50.2 216.0 %copy-start.4 = (bf16[384,864]{0,1:T(8,128)(2,1)S(1)}, bf16[384,864]{0,1:T(8,128)(2,1)}, u32[]{:S(2)}) copy-start(bf16[384,864]{0,1:T(8,128)(2,1)} %param.14) | copy-start | bytes 1990660
  266.2 56.3 %copy-start = (f32[864]{0:T(1024)S(1)}, f32[864]{0:T(1024)}, u32[]{:S(2)}) copy-start(f32[864]{0:T(1024)} %param.18) | copy-start | bytes 10372
  266.2 56.3 %copy-start.1 = (f32[864]{0:T(1024)S(1)}, f32[864]{0:T(1024)}, u32[]{:S(2)}) copy-start(f32[864]{0:T(1024)} %param.20) | copy-start | bytes 10372
Sparse Core Ops, SparseCore 0:
  10.1 78.6 all-gather.5
  91.8 61.9 all-gather.3
  156.0 80.5 all-gather.7
where the time goes:
time: 330 us
  blocking collectives  186 us (56%)
  waiting for transfers between devices  106 us (32%)
  between operations  17.1 us (5%)
  matrix products  16.4 us (5%)
  other arithmetic  4.6 us (1%)
    psum x1, blocking collectives, local(): head_data = lax.psum(head_part, ('dp', 'tensor'))  105 us
    all_gather x1, waiting for transfers between devices, local(): full_rows = lax.all_gather(dout, 'tensor', axis=0, tiled=True)  65 us
    psum x1, blocking collectives, local(): unit_data = lax.psum(unit_part, 'dp')  45.8 us
    all_gather x1, waiting for transfers between devices, local(): ctx_pre = contract(lax.all_gather(w_out, 'dp', axis=1, tiled=True))  38.7 us
    psum x1, blocking collectives, local(): unit_mass = lax.psum(local_mass, 'tensor')  34.9 us
    dot_general x2, matrix products, contract(): lax.dot_general(full_rows, piece, dims, preferred_element_type=jnp.float32)  15.9 us
  transfers between devices with their start and end apart: 3, of which 2 were waited for; matrix products, arithmetic and copies ran while one was open for 3% of the time, Pallas kernels for 0%

commit v1 on v0

--- a/solution.py
+++ b/solution.py
@@ -65,7 +65,11 @@
     p_head = open_prob(head_logits)
     p_unit = open_prob(unit_logits)
     local_mass = jnp.sum(p_unit)
-    unit_data = lax.psum(unit_part, "dp")
+    unit_data = unit_part
+    for hop in (1, 2, 4, 8, 16):
+        unit_data = unit_data + lax.ppermute(
+            unit_data, "dp", [(dev, dev ^ hop) for dev in range(32)]
+        )
     head_data = lax.psum(head_part, ("dp", "tensor"))
     unit_mass = lax.psum(local_mass, "tensor")
     denom = 4.0 * HEAD * H + 3.0 * FF

time: 330 us -> 382 us (1.16)
  waiting for transfers between devices: 106 us -> 185 us
  blocking collectives: 186 us -> 137 us
  starting transfers between devices: 0.11 us -> 19.2 us
    all_gather x1, waiting for transfers between devices: 0.01 us -> 81.7 us  [local(): hid_pre = contract(lax.all_gather(w_down, 'dp', axis=1, tiled=True))]
    psum x1 -> x0, blocking collectives: 45.8 us -> none  [local(): unit_data = lax.psum(unit_part, 'dp')]
    all_gather x1, waiting for transfers between devices: 65 us -> 31.4 us  [local(): full_rows = lax.all_gather(dout, 'tensor', axis=0, tiled=True)]
    all_gather x1, waiting for transfers between devices: 38.7 us -> 58.2 us  [local(): ctx_pre = contract(lax.all_gather(w_out, 'dp', axis=1, tiled=True))]
    ppermute x0 -> x5, starting transfers between devices: none -> 19.1 us  [local(): lax.ppermute(unit_data, 'dp', [(dev, dev ^ hop) for dev in range(32)])]
    ppermute x0 -> x5, waiting for transfers between devices: none -> 11.5 us  [local(): lax.ppermute(unit_data, 'dp', [(dev, dev ^ hop) for dev in range(32)])]
  transfers between devices with their start and end apart: 3 -> 8, of which waited for: 2 -> 6; matrix products, arithmetic and copies ran while one was open for 3% -> 5% of each run, Pallas kernels for 0% -> 0%
where the time goes in v1:
time: 382 us; the launch traced here: 379 us
  waiting for transfers between devices  185 us (48%)
  blocking collectives  137 us (36%)
  starting transfers between devices  19.2 us (5%)
  between operations  17.1 us (4%)
  matrix products  16.4 us (4%)
  other arithmetic  4.61 us (1%)
    psum x1, blocking collectives, local(): head_data = lax.psum(head_part, ('dp', 'tensor'))  102 us
    all_gather x1, waiting for transfers between devices, local(): hid_pre = contract(lax.all_gather(w_down, 'dp', axis=1, tiled=True))  81.7 us
    all_gather x1, waiting for transfers between devices, local(): ctx_pre = contract(lax.all_gather(w_out, 'dp', axis=1, tiled=True))  58.2 us
    psum x1, blocking collectives, local(): unit_mass = lax.psum(local_mass, 'tensor')  35 us
    all_gather x1, waiting for transfers between devices, local(): full_rows = lax.all_gather(dout, 'tensor', axis=0, tiled=True)  31.4 us
    ppermute x5, starting transfers between devices, local(): lax.ppermute(unit_data, 'dp', [(dev, dev ^ hop) for dev in range(32)])  19.1 us
    dot_general x2, matrix products, contract(): lax.dot_general(full_rows, piece, dims, preferred_element_type=jnp.float32)  15.9 us
    ppermute x5, waiting for transfers between devices, local(): lax.ppermute(unit_data, 'dp', [(dev, dev ^ hop) for dev in range(32)])  11.5 us
  transfers between devices with their start and end apart: 8, of which 6 were waited for; matrix products, arithmetic and copies ran while one was open for 5% of the time, Pallas kernels for 0%

profile of v1, /device:TPU:1, one launch (start us, length us, event | category | flops | bytes accessed | tf_op | source)
XLA Modules:
  0.0 378.9 jit_solution(4247431754333246797)
XLA Ops:
  7.2 0.0 all-gather.4.cloned.1.call-start
  7.2 0.7 all-gather.4.cloned.1.call-update
  7.9 0.0 all-gather.8.cloned.1.call-start
  7.9 0.7 all-gather.8.cloned.1.call-update
  8.6 0.0 all-gather.6.cloned.1.call-start
  8.7 0.7 all-gather.6.cloned.1.call-update
  9.4 1.3 fusion.2
  10.7 35.0 %psum.15 = f32[]{:T(128)} all-reduce(f32[]{:T(128)} %get-tuple-element.11), channel_id=1, replica_groups=mesh['dp'=32,'tensor'=16] {'tensor'}, use_global_device_ids=true, to_apply=%region_4.5 | all-reduce | flops 1 | bytes 8 | tf_op jit(solution)/shard_map/psum | solution.py:74
  48.3 1.3 fusion.17
  50.2 31.4 %all-gather.4.cloned.1.call-done = bf16[384,5120]{1,0:T(8,128)(2,1)} async-done(((bf16[24,5120]{1,0:T(8,128)(2,1)}), bf16[384,5120]{1,0:T(8,128)(2,1)}) %all-gather.4.cloned.1.call-update) | async-done | bytes 3932176 | tf_op jit(solution)/shard_map/all_gather | solution.py:52
  81.6 81.7 %all-gather.8.cloned.1.call-done = bf16[864,5120]{0,1:T(8,128)(2,1)} async-done(((bf16[864,160]{0,1:T(8,128)(2,1)}), bf16[864,5120]{0,1:T(8,128)(2,1)}) %all-gather.8.cloned.1.call-update) | async-done | bytes 8847376 | tf_op jit(solution)/shard_map/all_gather | solution.py:59
  163.3 10.5 %multiply_reduce_fusion = (f32[864]{0:T(1024)S(1)}, bf16[384,864]{0,1:T(8,128)(2,1)}) fusion(bf16[384,864]{0,1:T(8,128)(2,1)} %param.14, f32[864]{0:T(1024)S(1)} %get-tuple-element.10, bf16[384,5120]{1,0:T(8,128)(2,1)} %all-gather.4.cloned.1.call-done, bf16[864,5120]{0,1:T(8,128)(2,1)} %all-gather.8.cloned.1.call-done), kind=kOutput, calls=%fused_computation | convolution fusion | flops 3399044352 | bytes 14113536 | tf_op jit(solution)/shard_map/dot_general | solution.py:56
  173.8 2.3 collective-permute-start
  176.2 58.2 %all-gather.6.cloned.1.call-done = bf16[320,5120]{0,1:T(8,128)(2,1)} async-done(((bf16[320,160]{0,1:T(8,128)(2,1)}), bf16[320,5120]{0,1:T(8,128)(2,1)}) %all-gather.6.cloned.1.call-update) | async-done | bytes 3276816 | tf_op jit(solution)/shard_map/all_gather | solution.py:58
  234.4 5.3 %multiply_reduce_fusion.1 = (f32[320]{0:T(512)S(1)}, f32[384,320]{0,1:T(8,128)S(1)}) fusion(bf16[384,320]{0,1:T(8,128)(2,1)S(1)} %copy-done.4, bf16[384,5120]{1,0:T(8,128)(2,1)} %all-gather.4.cloned.1.call-done, bf16[320,5120]{0,1:T(8,128)(2,1)} %all-gather.6.cloned.1.call-done), kind=kOutput, calls=%fused_computation.4 | convolution fusion | flops 1258659584 | bytes 7947520 | tf_op jit(solution)/shard_map/dot_general | solution.py:56
  239.7 0.0 collective-permute-done
  239.7 3.4 collective-permute-start.1
  243.1 0.2 convolution_bitcast_fusion
  243.4 101.9 %psum.14 = f32[40]{0:T(128)S(1)} all-reduce(f32[40]{0:T(128)S(1)} %convolution_bitcast_fusion), channel_id=1, replica_groups=mesh['dp'=32,'tensor'=16] {'dp','tensor'}, use_global_device_ids=true, to_apply=%region_1.2 | all-reduce | flops 40 | bytes 320 | tf_op jit(solution)/shard_map/psum | solution.py:73
  345.2 0.0 collective-permute-done.1
  345.2 1.9 collective-permute-start.2
  347.2 0.0 copy-done.2
  347.2 0.0 copy-done.3
  347.2 0.5 multiply_add_fusion.2
  347.7 2.8 collective-permute-done.2
  350.5 4.2 %collective-permute-start.3 = (f32[864]{0:T(1024)S(1)}, f32[864]{0:T(1024)S(1)}, u32[]{:S(2)}, u32[]{:S(2)}) collective-permute-start(f32[864]{0:T(1024)S(1)} %add.95), channel_id=1, source_target_pairs={{0,128},{16,144},{32,160},{48,176},{64,192},{80,208},{96,224},{112... | collective-permute-start | bytes 10376 | tf_op jit(solution)/shard_map/ppermute | solution.py:70
  354.7 0.3 convolution_reduce_fusion
  355.0 3.8 collective-permute-done.3
  358.7 7.3 %collective-permute-start.4 = (f32[864]{0:T(1024)S(1)}, f32[864]{0:T(1024)S(1)}, u32[]{:S(2)}, u32[]{:S(2)}) collective-permute-start(f32[864]{0:T(1024)S(1)} %add.96), channel_id=1, source_target_pairs={{0,256},{16,272},{32,288},{48,304},{64,320},{80,336},{96,352},{112... | collective-permute-start | bytes 10376 | tf_op jit(solution)/shard_map/ppermute | solution.py:70
  366.0 0.8 multiply_convert_fusion.1
  366.8 5.0 %collective-permute-done.4 = f32[864]{0:T(1024)S(1)} collective-permute-done((f32[864]{0:T(1024)S(1)}, f32[864]{0:T(1024)S(1)}, u32[]{:S(2)}, u32[]{:S(2)}) %collective-permute-start.4) | collective-permute-done | bytes 3488 | tf_op jit(solution)/shard_map/ppermute | solution.py:70
  371.8 0.6 multiply_add_fusion
  (14 shorter events, 0.0 us)
Async XLA Ops:
  7.2 74.4 %all-gather.4.cloned.1.call-start = ((), (), s32[]{:S(2)}) async-start(), calls=%async_computation | async-start | bytes 4177920 | tf_op jit(solution)/shard_map/all_gather | solution.py:52
  7.9 155.4 %all-gather.8.cloned.1.call-start = ((), (), s32[]{:S(2)}) async-start(), calls=%async_computation.2 | async-start | bytes 9461760 | tf_op jit(solution)/shard_map/all_gather | solution.py:59
  8.6 225.7 %all-gather.6.cloned.1.call-start = ((), (), s32[]{:S(2)}) async-start(), calls=%async_computation.1 | async-start | bytes 4055040 | tf_op jit(solution)/shard_map/all_gather | solution.py:58
  163.3 71.1 %copy-start.4 = (bf16[384,320]{0,1:T(8,128)(2,1)S(1)}, bf16[384,320]{0,1:T(8,128)(2,1)}, u32[]{:S(2)}) copy-start(bf16[384,320]{0,1:T(8,128)(2,1)} %param.13) | copy-start | bytes 737284
  173.8 173.3 %copy-start.2 = (f32[40]{0:T(128)S(1)}, f32[40]{0:T(128)}, u32[]{:S(2)}) copy-start(f32[40]{0:T(128)} %param.17) | copy-start | bytes 484
  173.8 173.3 %copy-start.3 = (f32[40]{0:T(128)S(1)}, f32[40]{0:T(128)}, u32[]{:S(2)}) copy-start(f32[40]{0:T(128)} %param.19) | copy-start | bytes 484
  173.8 198.0 %copy-start = (f32[864]{0:T(1024)S(1)}, f32[864]{0:T(1024)}, u32[]{:S(2)}) copy-start(f32[864]{0:T(1024)} %param.18) | copy-start | bytes 10372
  173.8 198.0 %copy-start.1 = (f32[864]{0:T(1024)S(1)}, f32[864]{0:T(1024)}, u32[]{:S(2)}) copy-start(f32[864]{0:T(1024)} %param.20) | copy-start | bytes 10372
  173.8 65.9 %collective-permute-start = (f32[864]{0:T(1024)S(1)}, f32[864]{0:T(1024)S(1)}, u32[]{:S(2)}, u32[]{:S(2)}) collective-permute-start(f32[864]{0:T(1024)S(1)} %get-tuple-element.8), channel_id=1, source_target_pairs={{0,16},{16,0},{32,48},{48,32},{64,80},{80,64},{96,112},{112,96},{1... | collective-permute-start | bytes 10376 | tf_op jit(solution)/shard_map/ppermute | solution.py:70
  239.7 105.5 %collective-permute-start.1 = (f32[864]{0:T(1024)S(1)}, f32[864]{0:T(1024)S(1)}, u32[]{:S(2)}, u32[]{:S(2)}) collective-permute-start(f32[864]{0:T(1024)S(1)} %add.93), channel_id=1, source_target_pairs={{0,32},{16,48},{32,0},{48,16},{64,96},{80,112},{96,64},{112,80},{1... | collective-permute-start | bytes 10376 | tf_op jit(solution)/shard_map/ppermute | solution.py:70
  345.2 5.2 %collective-permute-start.2 = (f32[864]{0:T(1024)S(1)}, f32[864]{0:T(1024)S(1)}, u32[]{:S(2)}, u32[]{:S(2)}) collective-permute-start(f32[864]{0:T(1024)S(1)} %add.94), channel_id=1, source_target_pairs={{0,64},{16,80},{32,96},{48,112},{64,0},{80,16},{96,32},{112,48},{1... | collective-permute-start | bytes 10376 | tf_op jit(solution)/shard_map/ppermute | solution.py:70
  350.5 8.2 %collective-permute-start.3 = (f32[864]{0:T(1024)S(1)}, f32[864]{0:T(1024)S(1)}, u32[]{:S(2)}, u32[]{:S(2)}) collective-permute-start(f32[864]{0:T(1024)S(1)} %add.95), channel_id=1, source_target_pairs={{0,128},{16,144},{32,160},{48,176},{64,192},{80,208},{96,224},{112... | collective-permute-start | bytes 10376 | tf_op jit(solution)/shard_map/ppermute | solution.py:70
  358.7 13.1 %collective-permute-start.4 = (f32[864]{0:T(1024)S(1)}, f32[864]{0:T(1024)S(1)}, u32[]{:S(2)}, u32[]{:S(2)}) collective-permute-start(f32[864]{0:T(1024)S(1)} %add.96), channel_id=1, source_target_pairs={{0,256},{16,272},{32,288},{48,304},{64,320},{80,336},{96,352},{112... | collective-permute-start | bytes 10376 | tf_op jit(solution)/shard_map/ppermute | solution.py:70
Sparse Core Ops, SparseCore 0:
  11.0 70.5 all-gather.3
  83.7 79.5 all-gather.7
  165.4 68.8 all-gather.5
